TPU v7x, 32 devices: a whole 2x2x4 slice. The times are simulated.
32 devices in a mesh: dp: 2 (over core), node: 4 (over z), local: 4 (over y, x).
Axes of the slice: x: 2, y: 2, z: 4, core: 2. Of those that a mesh axis runs over, the one named last changes fastest.
Arguments:
- tokens: bfloat16 [4096, 3584], P(('dp', 'node', 'local')), parts along dimension 0, may hold values from -6 to 6
- gate_scores: float32 [4096, 4], P(('dp', 'node', 'local')), parts along dimension 0, may hold values from 0.1 to 1
- expert_ids: int32 [4096, 4], P(('dp', 'node', 'local')), parts along dimension 0, may hold values from 0 to 15, as said below
- w_gate: bfloat16 [16, 3584, 1024], P(('node', 'local')), may hold values from -0.09375 to 0.09375
- w_up: bfloat16 [16, 3584, 1024], P(('node', 'local')), may hold values from -0.09375 to 0.09375
- w_down: bfloat16 [16, 1024, 3584], P(('node', 'local')), may hold values from -0.1875 to 0.1875
Outputs:
- mixed: bfloat16 [4096, 3584], P(('dp', 'node', 'local')), parts along dimension 0
There are 2 independent parts, one for each index of `dp`. A program takes and returns all parts, laid end to end along the dimension named above; an argument that names none is the same for every part. Nothing has to cross between parts.
Inputs may be any that keep to these rules, and one draw needn't show every extreme that they name: `expert_ids`: expert e belongs to node group e // 4 and lives on the device of index e along node and local together. Each token names 4 different experts in exactly 2 different node groups, at least one in each. The 128 tokens of one device name every node group exactly 64 times, and in every node group one expert is named by all 64 of them, so no expert is named more than 64 times by the tokens of one device.
All inputs are finite; a program needn't handle non-finite values.
Results may differ from a plain program's by a relative error of at most 0.0075.
Values may be sent and summed in bfloat16 or wider, within the bound.
A program may use at most 192 MiB of HBM per device.

v0:
```python
import functools

import jax
import jax.numpy as jnp
from jax import lax
from jax.experimental import pallas as pl
from jax.experimental.pallas import tpu as pltpu
from jax.sharding import PartitionSpec as P

MAXNODES = 2
MESH = pl.DeviceIdType.MESH
LANES = 128


def kernel(
    nodes,
    tokens_ref, ids_ref, score_ref, wg_ref, wu_ref, wd_ref,
    out_ref,
    pick_ref, gate_ref, wg, wu, wd, sent, tok, gts, hid, part, rx, ry, dg0, dg1, ret,
    w_sem, ssem, rsem, gssem, grsem,
):
    group, cap, width = tok.shape[1:]
    half = (width // LANES // 2) * LANES
    node = lax.axis_index("node")
    local = lax.axis_index("local")
    low, high = pl.ds(0, half), pl.ds(half, width - half)
    x_dev, y_dev = {"local": local ^ 1}, {"local": local ^ 2}

    def remote(k, which, src, dst, dev):
        return pltpu.make_async_remote_copy(
            src_ref=src, dst_ref=dst, send_sem=ssem.at[which, k], recv_sem=rsem.at[which, k],
            device_id=dev, device_id_type=MESH,
        )

    def copies(k):
        z_dev = {"node": node ^ k}
        return [
            lambda: remote(k, 0, sent.at[k, :, low], tok.at[k, 0, :, low], z_dev),
            lambda: remote(k, 1, tok.at[k, 0, :, low], tok.at[k, 1, :, low], x_dev),
            lambda: remote(k, 2, tok.at[k, 0, :, high], tok.at[k, 1, :, high], x_dev),
            lambda: remote(k, 3, tok.at[k, 0, :, high], tok.at[k, 2, :, high], y_dev),
            lambda: remote(k, 4, tok.at[k, 0, :, low], tok.at[k, 2, :, low], y_dev),
            lambda: remote(k, 5, tok.at[k, 1, :, low], tok.at[k, 3, :, low], y_dev),
            lambda: remote(k, 6, tok.at[k, 2, :, high], tok.at[k, 3, :, high], x_dev),
            lambda: remote(k, 7, part.at[k, 3, :, low], dg0.at[k], y_dev),
            lambda: remote(k, 8, part.at[k, 3, :, high], dg1.at[k], x_dev),
            lambda: remote(k, 9, part.at[k, 1, :, high], rx.at[k, :, high], x_dev),
            lambda: remote(k, 10, part.at[k, 2, :, low], ry.at[k, :, low], y_dev),
            lambda: remote(k, 11, part.at[k, 1, :, low], rx.at[k, :, low], x_dev),
            lambda: remote(k, 12, part.at[k, 2, :, high], ry.at[k, :, high], y_dev),
            lambda: remote(k, 13, part.at[k, 0, :, low], ret.at[k, :, low], z_dev),
            lambda: remote(k, 14, sent.at[k, :, high], tok.at[k, 0, :, high], z_dev),
            lambda: remote(k, 15, part.at[k, 0, :, high], ret.at[k, :, high], z_dev),
        ]

    def start(k, *which):
        for i in which:
            copies(k)[i]().start()

    def arrived(k, *which):
        for i in which:
            copies(k)[i]().wait_recv()

    def gate_copy(k, r):
        return pltpu.make_async_remote_copy(
            src_ref=gate_ref.at[k], dst_ref=gts.at[k, r],
            send_sem=gssem.at[k, r], recv_sem=grsem.at[k, r],
            device_id={"node": node ^ k, "local": local ^ r}, device_id_type=MESH,
        )

    def spread(k):
        arrived(k, 0)
        start(k, 1, 4)
        arrived(k, 14)
        start(k, 3, 2)

    def forward(k):
        arrived(k, 1)
        start(k, 5)
        arrived(k, 3)
        start(k, 6)

    def up(k):
        rows = tok[k].reshape(group * cap, width)
        tile = 256

        @pl.loop(0, wg.shape[1] // tile)
        def _(j):
            cols = pl.ds(pl.multiple_of(j * tile, tile), tile)
            a = jnp.dot(rows, wg[:, cols], preferred_element_type=jnp.float32)
            b = jnp.dot(rows, wu[:, cols], preferred_element_type=jnp.float32)
            hid[:, cols] = (a / (1.0 + jnp.exp(-a)) * b).astype(jnp.bfloat16)

    def down(k):
        gates = gts[k].astype(jnp.float32)
        row = lax.broadcasted_iota(jnp.int32, gates.shape, 1)
        flat = jnp.sum(jnp.where(row == local, gates, 0.0), axis=1, keepdims=True)
        wide = jnp.broadcast_to(flat, (group, cap, LANES))
        slot = lax.broadcasted_iota(jnp.int32, wide.shape, 1)
        lane = lax.broadcasted_iota(jnp.int32, wide.shape, 2)
        mine = jnp.sum(jnp.where(slot == lane, wide, 0.0), axis=2, keepdims=True)
        tile = 512

        @pl.loop(0, width // tile)
        def _(j):
            cols = pl.ds(pl.multiple_of(j * tile, tile), tile)
            y = jnp.dot(hid[...], wd[:, cols], preferred_element_type=jnp.float32)
            part[k, :, :, cols] = (y.reshape(group, cap, tile) * mine).astype(jnp.bfloat16)

    def add(a, b):
        return (a.astype(jnp.float32) + b.astype(jnp.float32)).astype(jnp.bfloat16)

    def give(k):
        start(k, 7, 8, 10, 9)

    def relay(k):
        arrived(k, 7)
        part[k, 1, :, low] = add(part[k, 1, :, low], dg0[k])
        start(k, 11)
        arrived(k, 8)
        part[k, 2, :, high] = add(part[k, 2, :, high], dg1[k])
        start(k, 12)

    def settle(k, cols):
        arrived(k, *((10, 11) if cols is low else (9, 12)))
        return (
            part[k, 0, :, cols].astype(jnp.float32)
            + rx[k, :, cols].astype(jnp.float32)
            + ry[k, :, cols].astype(jnp.float32)
        ).astype(jnp.bfloat16)

    def finish(k):
        part[k, 0, :, low] = settle(k, low)
        start(k, 13)
        part[k, 0, :, high] = settle(k, high)
        start(k, 15)

    w_copies = [
        pltpu.make_async_copy(wg_ref.at[0], wg, w_sem.at[0]),
        pltpu.make_async_copy(wu_ref.at[0], wu, w_sem.at[1]),
        pltpu.make_async_copy(wd_ref.at[0], wd, w_sem.at[2]),
    ]
    others = [(k, r) for k in range(nodes) for r in range(group) if (k, r) != (0, 0)]
    barrier = pltpu.get_barrier_semaphore()
    for k, r in others:
        pl.semaphore_signal(
            barrier, inc=1, device_id={"node": node ^ k, "local": local ^ r}, device_id_type=MESH
        )

    step = 2 * LANES

    def restore(first, count):
        @pl.loop(first, first + count)
        def _(j):
            cols = pl.ds(pl.multiple_of(j * step, step), step)
            x = tokens_ref[:, cols].astype(jnp.float32)
            tiles = []
            for t in range(2):
                v = x[:, t * LANES:(t + 1) * LANES]
                largest = jnp.max(jnp.abs(v), axis=1, keepdims=True)
                scale = ((largest + 1e-06) / 448.0).astype(jnp.bfloat16).astype(jnp.float32)
                quantized = (v / scale).astype(jnp.bfloat16).astype(jnp.float32)
                tiles.append((quantized * scale).astype(jnp.bfloat16))
            chosen = jnp.dot(
                pick_ref[...], jnp.concatenate(tiles, axis=1), preferred_element_type=jnp.float32
            ).astype(jnp.bfloat16)
            tok[0, 0, :, cols] = chosen[:cap]
            sent[:, :, cols] = chosen.reshape(nodes, cap, step)

    rows = tokens_ref.shape[0]
    ids = ids_ref[...]
    score = score_ref[...]
    gates = (2.5 * score / jnp.sum(score, axis=0, keepdims=True)).astype(jnp.bfloat16)
    gates = gates.astype(jnp.float32)
    before = (
        lax.broadcasted_iota(jnp.int32, (rows, rows), 0)
        < lax.broadcasted_iota(jnp.int32, (rows, rows), 1)
    ).astype(jnp.float32).astype(jnp.bfloat16)
    for k in range(nodes):
        sums = [
            jnp.sum(jnp.where(ids == (node ^ k) * group + r, 1.0, 0.0), axis=0, keepdims=True)
            for r in range(group)
        ]
        weights = [
            jnp.sum(jnp.where(ids == (node ^ k) * group + r, gates, 0.0), axis=0, keepdims=True)
            for r in range(group)
        ]
        hit = jnp.minimum(functools.reduce(lambda a, b: a + b, sums), 1.0)
        rank = jnp.dot(
            jnp.broadcast_to(hit, (16, rows)).astype(jnp.bfloat16), before,
            preferred_element_type=jnp.float32,
        )[0:1].astype(jnp.int32)
        slot = lax.broadcasted_iota(jnp.int32, (LANES, rows), 0)
        chosen = jnp.where((slot == rank) & (slot < cap), hit, 0.0)
        line = lax.broadcasted_iota(jnp.int32, (16, rows), 0)
        table = jnp.zeros((16, rows), jnp.float32)
        for r in range(group):
            table = jnp.where(line == r, weights[r], table)
        chosen = chosen.astype(jnp.bfloat16)
        pick_ref[k * cap:(k + 1) * cap] = chosen[:cap]
        gate_ref[k] = lax.dot_general(
            table.astype(jnp.bfloat16), chosen, (((1,), (1,)), ((), ())),
            preferred_element_type=jnp.float32,
        ).astype(jnp.bfloat16)
    gts[0, 0] = gate_ref[0]
    restore(0, half // step)
    pl.semaphore_wait(barrier, nodes * group - 1)
    start(0, 1, 4)
    for k in range(1, nodes):
        start(k, 0)
    restore(half // step, (width - half) // step)
    start(0, 3, 2)
    for k in range(1, nodes):
        start(k, 14)
    for k, r in others:
        gate_copy(k, r).start()
    for c in w_copies:
        c.start()
    forward(0)

    for k in range(nodes):
        if k + 1 < nodes:
            spread(k + 1)
        arrived(k, 2, 4, 5, 6)
        if k == 0:
            w_copies[0].wait()
            w_copies[1].wait()
        up(k)
        if k + 1 < nodes:
            forward(k + 1)
        if k == 0:
            w_copies[2].wait()
        for r in range(group):
            if (k, r) != (0, 0):
                gate_copy(k, r).wait_recv()
        down(k)
        if k >= 3:
            relay(k - 1)
        if k >= 2:
            give(k)
        if k >= 4:
            finish(k - 2)
    give(1)
    relay(nodes - 1)
    finish(nodes - 2)
    relay(1)
    give(0)
    finish(nodes - 1)
    finish(1)
    relay(0)
    ret[0, :, low] = settle(0, low)
    ret[0, :, high] = settle(0, high)

    @pl.loop(1, nodes)
    def _(k):
        arrived(k, 13, 15)

    tile = 512
    blocks = nodes * cap

    @pl.loop(0, width // tile)
    def _(j):
        cols = pl.ds(pl.multiple_of(j * tile, tile), tile)
        vals = ret[:, :, cols].reshape(blocks, tile)
        out_ref[:, cols] = lax.dot_general(
            pick_ref[...], vals, (((0,), (0,)), ((), ())), preferred_element_type=jnp.float32
        ).astype(jnp.bfloat16)

    for i in range(1, 13):
        @pl.loop(0, nodes)
        def _(k):
            copies(k)[i]().wait_send()

    for k, r in others:
        gate_copy(k, r).wait_send()

    for i in (0, 13, 14, 15):
        @pl.loop(1, nodes)
        def _(k):
            copies(k)[i]().wait_send()


def per_device(tokens, gate_scores, expert_ids, w_gate, w_up, w_down):
    rows, width = tokens.shape
    nodes = lax.axis_size("node")
    group = lax.axis_size("local")
    cap = MAXNODES * rows // nodes
    hidden = w_gate.shape[2]

    half = (width // LANES // 2) * LANES
    bf16 = jnp.bfloat16
    anywhere = pl.BlockSpec(memory_space=pl.ANY)
    vmem = pl.BlockSpec(memory_space=pltpu.VMEM)
    pairs = nodes * group * cap
    return pl.pallas_call(
        functools.partial(kernel, nodes),
        out_shape=jax.ShapeDtypeStruct((rows, width), bf16),
        in_specs=[vmem] * 3 + [anywhere] * 3,
        out_specs=vmem,
        scratch_shapes=[
            pltpu.VMEM((nodes * cap, rows), bf16),
            pltpu.VMEM((nodes, 16, LANES), bf16),
            pltpu.VMEM((width, hidden), bf16),
            pltpu.VMEM((width, hidden), bf16),
            pltpu.VMEM((hidden, width), bf16),
            pltpu.VMEM((nodes, cap, width), bf16),
            pltpu.VMEM((nodes, group, cap, width), bf16),
            pltpu.VMEM((nodes, group, 16, LANES), bf16),
            pltpu.VMEM((group * cap, hidden), bf16),
            pltpu.VMEM((nodes, group, cap, width), bf16),
            pltpu.VMEM((nodes, cap, width), bf16),
            pltpu.VMEM((nodes, cap, width), bf16),
            pltpu.VMEM((nodes, cap, half), bf16),
            pltpu.VMEM((nodes, cap, width - half), bf16),
            pltpu.VMEM((nodes, cap, width), bf16),
            pltpu.SemaphoreType.DMA((3,)),
            pltpu.SemaphoreType.DMA((16, nodes)),
            pltpu.SemaphoreType.DMA((16, nodes)),
            pltpu.SemaphoreType.DMA((nodes, group)),
            pltpu.SemaphoreType.DMA((nodes, group)),
        ],
        compiler_params=pltpu.CompilerParams(
            collective_id=0, has_side_effects=True, vmem_limit_bytes=67043328
        ),
        cost_estimate=pl.CostEstimate(
            flops=6 * pairs * width * hidden,
            bytes_accessed=6 * width * hidden,
            transcendentals=pairs * hidden,
        ),
        name="routed_experts",
    )(tokens, expert_ids.T, gate_scores.T, w_gate, w_up, w_down)


def solution(mesh):
    in_specs = (
        P(("dp", "node", "local"), None),
        P(("dp", "node", "local"), None),
        P(("dp", "node", "local"), None),
        P(("node", "local"), None, None),
        P(("node", "local"), None, None),
        P(("node", "local"), None, None),
    )
    out_specs = P(("dp", "node", "local"), None)
    return jax.shard_map(
        per_device, mesh=mesh, in_specs=in_specs, out_specs=out_specs, check_vma=False
    )
```

profile of v0, /device:TPU:0, one launch (start us, length us, event | category | flops | bytes accessed | tf_op | source)
XLA Modules:
  0.0 136.7 jit_solution(16105763621053616391)
XLA Ops:
  0.0 134.5 %routed_experts.1 = bf16[128,3584]{1,0:T(8,128)(2,1)} custom-call(bf16[128,3584]{1,0:T(8,128)(2,1)} %tokens_ref.1, s32[4,128]{1,0:T(4,128)} %bitcast.2, f32[4,128]{1,0:T(4,128)} %bitcast.3, bf16[1,3584,1024]{2,1,0:T(8,128)(2,1)} %wg_ref.1, bf16[1,3584,1024]{2,1,0:T(8,128)(2,1)} %wu_ref.1, bf16[1,1024,3584]{2,1,0:T(8,128)(2,1)} %wd_ref.1), custom_call_target="tpu_custom_call" | custom-call | flops 22548578304 | bytes 22020096 | tf_op jit(solution)/shard_map/routed_experts/pallas_call | solution.py:295
  134.6 2.2 %copy.8 = bf16[128,3584]{1,0:T(8,128)(2,1)} copy(bf16[128,3584]{1,0:T(8,128)(2,1)} %routed_experts.1) | data formatting | bytes 1835008
where the time goes:
time: 137 us
  Pallas kernels  135 us (99%)
  local copies, waits for them, and re-layouts  2.16 us (2%)
    pallas_call x1, Pallas kernels, per_device(): pl.pallas_call(functools.partial(kernel, nodes), out_shape=jax.ShapeDtype...  135 us

commit v1 on v0

--- a/solution.py
+++ b/solution.py
@@ -206,14 +206,15 @@
     restore(0, half // step)
     pl.semaphore_wait(barrier, nodes * group - 1)
     start(0, 1, 4)
-    for k in range(1, nodes):
-        start(k, 0)
-    restore(half // step, (width - half) // step)
-    start(0, 3, 2)
-    for k in range(1, nodes):
-        start(k, 14)
+    start(1, 0)
     for k, r in others:
         gate_copy(k, r).start()
+    restore(half // step, (width - half) // step)
+    start(1, 14)
+    start(0, 3, 2)
+    for k in range(2, nodes):
+        start(k, 0)
+        start(k, 14)
     for c in w_copies:
         c.start()
     forward(0)
@@ -294,7 +295,7 @@
     pairs = nodes * group * cap
     return pl.pallas_call(
         functools.partial(kernel, nodes),
-        out_shape=jax.ShapeDtypeStruct((rows, width), bf16),
+        out_shape=pltpu.VMEM((rows, width), bf16),
         in_specs=[vmem] * 3 + [anywhere] * 3,
         out_specs=vmem,
         scratch_shapes=[
@@ -320,7 +321,7 @@
             pltpu.SemaphoreType.DMA((nodes, group)),
         ],
         compiler_params=pltpu.CompilerParams(
-            collective_id=0, has_side_effects=True, vmem_limit_bytes=67043328
+            collective_id=0, has_side_effects=True, vmem_limit_bytes=56*2**20
         ),
         cost_estimate=pl.CostEstimate(
             flops=6 * pairs * width * hidden,

time: 137 us -> 134 us (0.978)
  Pallas kernels: 135 us -> 133 us
    pallas_call x1, Pallas kernels: 135 us -> 133 us  [per_device(): pl.pallas_call(functools.partial(kernel, nodes), out_shape=pltpu.VMEM((ro...]
where the time goes in v1:
time: 134 us
  Pallas kernels  133 us (99%)
    pallas_call x1, Pallas kernels, per_device(): pl.pallas_call(functools.partial(kernel, nodes), out_shape=pltpu.VMEM((ro...  133 us

profile of v1, /device:TPU:0, one launch (start us, length us, event | category | flops | bytes accessed | tf_op | source)
XLA Modules:
  0.0 133.6 jit_solution(9372597738472371058)
XLA Ops:
  0.0 132.7 %routed_experts.1 = bf16[128,3584]{1,0:T(8,128)(2,1)S(1)} custom-call(bf16[128,3584]{1,0:T(8,128)(2,1)} %tokens_ref.1, s32[4,128]{1,0:T(4,128)} %bitcast.2, f32[4,128]{1,0:T(4,128)} %bitcast.3, bf16[1,3584,1024]{2,1,0:T(8,128)(2,1)} %wg_ref.1, bf16[1,3584,1024]{2,1,0:T(8,128)(2,1)} %wu_ref.1, bf16[1,1024,3584]{2,1,0:T(8,128)(2,1)} %wd_ref.1), custom_call_target="tpu_custom_call" | custom-call | flops 22548578304 | bytes 22020096 | tf_op jit(solution)/shard_map/routed_experts/pallas_call | solution.py:296
  132.7 0.9 copy.8

commit v2 on v1

--- a/solution.py
+++ b/solution.py
@@ -241,31 +241,34 @@
             give(k)
         if k >= 4:
             finish(k - 2)
+    finish(nodes - 2)
+    relay(nodes - 1)
     give(1)
-    relay(nodes - 1)
-    finish(nodes - 2)
+    finish(nodes - 1)
     relay(1)
     give(0)
-    finish(nodes - 1)
     finish(1)
     relay(0)
-    ret[0, :, low] = settle(0, low)
-    ret[0, :, high] = settle(0, high)
 
     @pl.loop(1, nodes)
     def _(k):
         arrived(k, 13, 15)
 
     tile = 512
-    blocks = nodes * cap
+    flipped = pick_ref[...].astype(jnp.float32).T.astype(jnp.bfloat16)
+    own_pick, far_pick = flipped[:, :cap], flipped[:, cap:]
 
     @pl.loop(0, width // tile)
     def _(j):
         cols = pl.ds(pl.multiple_of(j * tile, tile), tile)
-        vals = ret[:, :, cols].reshape(blocks, tile)
-        out_ref[:, cols] = lax.dot_general(
-            pick_ref[...], vals, (((0,), (0,)), ((), ())), preferred_element_type=jnp.float32
+        vals = ret[1:, :, cols].reshape((nodes - 1) * cap, tile)
+        out_ref[:, cols] = jnp.dot(
+            far_pick, vals, preferred_element_type=jnp.float32
         ).astype(jnp.bfloat16)
+
+    for cols in (low, high):
+        own = jnp.dot(own_pick, settle(0, cols), preferred_element_type=jnp.float32)
+        out_ref[:, cols] = (out_ref[:, cols].astype(jnp.float32) + own).astype(jnp.bfloat16)
 
     for i in range(1, 13):
         @pl.loop(0, nodes)

time: 134 us -> 132 us (0.985)
  Pallas kernels: 133 us -> 131 us
where the time goes in v2:
time: 132 us
  Pallas kernels  131 us (99%)
    pallas_call x1, Pallas kernels, per_device(): pl.pallas_call(functools.partial(kernel, nodes), out_shape=pltpu.VMEM((ro...  131 us

profile of v2, /device:TPU:0, one launch (start us, length us, event | category | flops | bytes accessed | tf_op | source)
XLA Modules:
  0.0 132.3 jit_solution(4413171400212164106)
XLA Ops:
  0.0 131.4 %routed_experts.1 = bf16[128,3584]{1,0:T(8,128)(2,1)S(1)} custom-call(bf16[128,3584]{1,0:T(8,128)(2,1)} %tokens_ref.1, s32[4,128]{1,0:T(4,128)} %bitcast.2, f32[4,128]{1,0:T(4,128)} %bitcast.3, bf16[1,3584,1024]{2,1,0:T(8,128)(2,1)} %wg_ref.1, bf16[1,3584,1024]{2,1,0:T(8,128)(2,1)} %wu_ref.1, bf16[1,1024,3584]{2,1,0:T(8,128)(2,1)} %wd_ref.1), custom_call_target="tpu_custom_call" | custom-call | flops 22548578304 | bytes 22020096 | tf_op jit(solution)/shard_map/routed_experts/pallas_call | solution.py:299
  131.4 0.9 copy.8

commit v3 on v2

--- a/solution.py
+++ b/solution.py
@@ -23,6 +23,7 @@
     half = (width // LANES // 2) * LANES
     node = lax.axis_index("node")
     local = lax.axis_index("local")
+    core = lax.axis_index("dp")
     low, high = pl.ds(0, half), pl.ds(half, width - half)
     x_dev, y_dev = {"local": local ^ 1}, {"local": local ^ 2}
 
@@ -227,6 +228,11 @@
             w_copies[0].wait()
             w_copies[1].wait()
         up(k)
+        if k + 1 == nodes - 1:
+            @pl.when(core == 0)
+            def _():
+                start(1, 7, 8)
+
         if k + 1 < nodes:
             forward(k + 1)
         if k == 0:
@@ -243,7 +249,12 @@
             finish(k - 2)
     finish(nodes - 2)
     relay(nodes - 1)
-    give(1)
+    start(1, 10, 9)
+
+    @pl.when(core == 1)
+    def _():
+        start(1, 7, 8)
+
     finish(nodes - 1)
     relay(1)
     give(0)

time: 132 us -> 132 us (level)
  no operation moved by 1% of the time
where the time goes in v3:
time: 132 us
  Pallas kernels  131 us (99%)
    pallas_call x1, Pallas kernels, per_device(): pl.pallas_call(functools.partial(kernel, nodes), out_shape=pltpu.VMEM((ro...  131 us

profile of v3, /device:TPU:0, one launch (start us, length us, event | category | flops | bytes accessed | tf_op | source)
XLA Modules:
  0.0 132.0 jit_solution(6683753854724504916)
XLA Ops:
  0.0 131.0 %routed_experts.1 = bf16[128,3584]{1,0:T(8,128)(2,1)S(1)} custom-call(bf16[128,3584]{1,0:T(8,128)(2,1)} %tokens_ref.1, s32[4,128]{1,0:T(4,128)} %bitcast.2, f32[4,128]{1,0:T(4,128)} %bitcast.3, bf16[1,3584,1024]{2,1,0:T(8,128)(2,1)} %wg_ref.1, bf16[1,3584,1024]{2,1,0:T(8,128)(2,1)} %wu_ref.1, bf16[1,1024,3584]{2,1,0:T(8,128)(2,1)} %wd_ref.1), custom_call_target="tpu_custom_call" | custom-call | flops 22548578304 | bytes 22020096 | tf_op jit(solution)/shard_map/routed_experts/pallas_call | solution.py:310
  131.0 0.9 copy.8
